TPU v7x, 256 devices: a whole 4x4x8 slice. The times are simulated.
256 devices in a mesh: teach: 4 (over x), vocab: 64 (over z, y, core), tok: 1.
Axes of the slice: x: 4, y: 4, z: 8, core: 2. Of those that a mesh axis runs over, the one named last changes fastest.
Arguments:
- teacher_logits: bfloat16 [4, 2048, 128256], P('teach', 'tok', 'vocab'), may hold values from -300 to 300
- teacher_weight: float32 [4], P('teach'), may hold values from 0.5 to 4
- student_logits: bfloat16 [2048, 128256], P(('tok', 'teach'), 'vocab'), may hold values from -300 to 300
Outputs:
- divergence: float32 [2048], P(('tok', 'teach'))
All inputs are finite; a program needn't handle non-finite values.
Results may differ from a plain program's by a relative error of at most 0.0035.
Values may be sent and summed in bfloat16 or wider, within the bound.
A program may use at most 64 MiB of HBM per device.

v0:
```python
import jax
import jax.numpy as jnp
from jax import lax
from jax.sharding import PartitionSpec as P


def sent_to_all(array, axis):
    copies = jnp.broadcast_to(array, (lax.axis_size(axis), *array.shape))
    return lax.all_to_all(copies, axis, split_axis=0, concat_axis=0, tiled=True)


def combined_pairwise(pieces, combine):
    while len(jax.tree.leaves(pieces)[0]) > 1:
        pieces = jax.vmap(combine)(
            *(jax.tree.map(lambda part: part[side::2], pieces) for side in (0, 1))
        )
    return jax.tree.map(lambda part: part[0], pieces)


def joined_all(array, axis, combine):
    pieces = jax.tree.map(lambda part: sent_to_all(part, axis), array)
    return combined_pairwise(pieces, combine)


def joined_along(blocks, dim):
    lengths = list(blocks.shape[1:])
    lengths[dim] *= blocks.shape[0]
    return jnp.moveaxis(blocks, 0, dim).reshape(lengths)


def gather_directly(array, axis, dim):
    blocks = sent_to_all(array, axis)
    return joined_along(blocks, dim)


def of_everyone(array, axis):
    everything = sent_to_all(array, axis)
    return jnp.sum(everything, axis=0)


def combine_pairs(earlier, later):
    peak = jnp.maximum(earlier[0], later[0])
    total = earlier[1] * jnp.exp(earlier[0] - peak) + later[1] * jnp.exp(later[0] - peak)
    return (peak, total)


def merge_both(first, second):
    return (combine_pairs(first[0], second[0]), combine_pairs(first[1], second[1]))


def local(teacher_logits, teacher_weight, student_logits):
    scores = teacher_logits[0]
    local_peak = jnp.max(scores, axis=1).astype(jnp.float32)
    student_local = jnp.max(student_logits, axis=1).astype(jnp.float32)
    teacher_part = jnp.sum(jnp.exp(scores.astype(jnp.float32) - local_peak[:, None]), axis=1)
    student_part = jnp.sum(
        jnp.exp(student_logits.astype(jnp.float32) - student_local[:, None]), axis=1
    )
    merged = joined_all(
        ((local_peak, teacher_part), (student_local, student_part)), "vocab", merge_both
    )
    peak, total = merged[0]
    student_peak, student_total = merged[1]
    weights_all = gather_directly(teacher_weight, "teach", 0)
    share = teacher_weight[0] / jnp.sum(weights_all)
    block = scores.astype(jnp.float32)
    mixture = lax.psum_scatter(
        (share * (jnp.exp(block - peak[:, None]) / total[:, None])).astype(jnp.bfloat16),
        "teach",
        scatter_dimension=0,
        tiled=True,
    ).astype(jnp.float32)
    logq = (
        student_logits.astype(jnp.float32) - student_peak[:, None] - jnp.log(student_total)[:, None]
    )
    safe = jnp.maximum(mixture, 1e-30)
    partial_value = jnp.sum(mixture * (jnp.log(safe) - logq), axis=1)
    return of_everyone(partial_value, "vocab")


def solution(mesh):
    in_specs = (P("teach", "tok", "vocab"), P("teach"), P(("tok", "teach"), "vocab"))
    out_specs = P(("tok", "teach"))
    return jax.shard_map(local, mesh=mesh, in_specs=in_specs, out_specs=out_specs, check_vma=False)
```

profile of v0, /device:TPU:1, one launch (start us, length us, event | category | flops | bytes accessed | tf_op | source)
XLA Modules:
  0.0 199.4 jit_solution(3305271275718692907)
XLA Ops:
  7.2 0.6 broadcast_in_dim.21
  7.8 4.8 %all-to-all-start = ((f32[4,1,1]{2,1,0:T(1,128)}), f32[4,1,1]{2,1,0:T(1,128)S(1)}, u32[]{:S(2)}, u32[]{:S(2)}) async-start(f32[4,1,1]{2,1,0:T(1,128)} %broadcast_in_dim.21), calls=%async_computation | async-start | bytes 4096 | tf_op jit(solution)/shard_map/all_to_all | solution.py:9
  12.6 4.7 %reduce_max.18 = bf16[2048]{0:T(1024)(128)(2,1)S(1)} reduce(bf16[1,2048,2004]{1,2,0:T(8,128)(2,1)} %param.3, bf16[]{:T(256)} %constant.1.clone.1), dimensions={0,2}, to_apply=%region_1.0 | reduce | flops 4102144 | bytes 8212482 | tf_op jit(solution)/shard_map/reduce_max | solution.py:53
  17.3 6.1 %fusion.5 = f32[2048]{0:T(1024)S(1)} fusion(bf16[1,2048,2004]{1,2,0:T(8,128)(2,1)} %param.3, f32[2048]{0:T(1024)S(1)} %convert_element_type.33), kind=kLoop, calls=%fused_computation.7 | loop fusion | flops 12310528 | bytes 8224768 | tf_op jit(solution)/shard_map/reduce_sum | solution.py:55
  23.4 0.3 broadcast_in_dim.23
  23.7 30.1 %all_to_all.48 = f32[64,1,2048]{2,1,0:T(1,128)S(1)} all-to-all(f32[64,1,2048]{2,1,0:T(1,128)S(1)} %broadcast_in_dim.23), channel_id=1, replica_groups=mesh['teach'=4,'vocab'=64,'tok'=1] {'vocab'}, dimensions={0} | all-to-all | bytes 1048576 | tf_op jit(solution)/shard_map/all_to_all | solution.py:9
  53.8 1.1 broadcast_in_dim.22
  54.8 5.7 %all-to-all-start.1 = ((f32[64,1,2048]{2,1,0:T(1,128)}), f32[64,1,2048]{2,1,0:T(1,128)S(1)}, u32[]{:S(2)}, u32[]{:S(2)}) async-start(f32[64,1,2048]{2,1,0:T(1,128)} %broadcast_in_dim.22), calls=%async_computation.1 | async-start | bytes 1048576 | tf_op jit(solution)/shard_map/all_to_all | solution.py:9
  60.6 0.6 reduce_sum.45
  61.9 0.2 copy.16
  62.4 15.9 %all-to-all-done.1 = f32[64,1,2048]{2,1,0:T(1,128)S(1)} async-done(((f32[64,1,2048]{2,1,0:T(1,128)}), f32[64,1,2048]{2,1,0:T(1,128)S(1)}, u32[]{:S(2)}, u32[]{:S(2)}) %all-to-all-start.1) | async-done | bytes 524320 | tf_op jit(solution)/shard_map/all_to_all | solution.py:9
  78.3 0.2 copy.17
  79.7 8.6 %fusion.3 = bf16[2048,2004]{0,1:T(8,128)(2,1)} fusion(bf16[1,2048,2004]{1,2,0:T(8,128)(2,1)} %param.3, f32[2048]{0:T(1024)S(1)} %bitcast.31, f32[2048]{0:T(1024)S(1)} %bitcast.32, f32[]{:T(128)S(6)} %div.13), kind=kLoop, calls=%fused_computation.5 | loop fusion | flops 20520960 | bytes 16433156 | tf_op jit(solution)/shard_map/convert_element_type | solution.py:68
  88.3 1.6 copy-done
  89.9 0.3 reduce_max.19
  90.2 0.7 fusion.11
  91.0 16.6 %all_to_all.49 = f32[64,1,512]{2,1,0:T(1,128)S(1)} all-to-all(f32[64,1,512]{2,1,0:T(1,128)S(1)} %broadcast_in_dim.25), channel_id=1, replica_groups=mesh['teach'=4,'vocab'=64,'tok'=1] {'vocab'}, dimensions={0} | all-to-all | bytes 262144 | tf_op jit(solution)/shard_map/all_to_all | solution.py:9
  107.7 0.7 broadcast_in_dim.24
  108.4 4.6 %all-to-all-start.3 = ((f32[64,1,512]{2,1,0:T(1,128)}), f32[64,1,512]{2,1,0:T(1,128)S(1)}, u32[]{:S(2)}, u32[]{:S(2)}) async-start(f32[64,1,512]{2,1,0:T(1,128)} %broadcast_in_dim.24), calls=%async_computation.4 | async-start | bytes 262144 | tf_op jit(solution)/shard_map/all_to_all | solution.py:9
  113.1 11.3 %all-to-all-done.3 = f32[64,1,512]{2,1,0:T(1,128)S(1)} async-done(((f32[64,1,512]{2,1,0:T(1,128)}), f32[64,1,512]{2,1,0:T(1,128)S(1)}, u32[]{:S(2)}, u32[]{:S(2)}) %all-to-all-start.3) | async-done | bytes 131104 | tf_op jit(solution)/shard_map/all_to_all | solution.py:9
  125.0 42.3 %reduce-scatter.2.cloned.1.call-done = bf16[512,2004]{0,1:T(8,128)(2,1)} async-done(((bf16[2048,2004]{0,1:T(8,128)(2,1)}), bf16[512,2004]{0,1:T(8,128)(2,1)}) %reduce-scatter.2.cloned.1.call-update) | async-done | bytes 2052112 | tf_op jit(solution)/shard_map/reduce_scatter | solution.py:67
  167.3 2.9 %fusion.8 = f32[512]{0:T(512)S(1)} fusion(bf16[512,2004]{0,1:T(8,128)(2,1)} %reduce-scatter.2.cloned.1.call-done, bf16[512,2004]{0,1:T(8,128)(2,1)S(1)} %copy-done, f32[512]{0:T(512)S(1)} %bitcast.33, f32[512]{0:T(512)S(1)} %bitcast.34), kind=kLoop, calls=%fused_computation.14 | loop fusion | flops 8207872 | bytes 4110336 | tf_op jit(solution)/shard_map/reduce_sum | solution.py:77
  170.3 21.5 %all_to_all.50 = f32[64,1,512]{2,1,0:T(1,128)S(1)} all-to-all(f32[64,1,512]{2,1,0:T(1,128)S(1)} %broadcast_in_dim.26), channel_id=1, replica_groups=mesh['teach'=4,'vocab'=64,'tok'=1] {'vocab'}, dimensions={0} | all-to-all | bytes 262144 | tf_op jit(solution)/shard_map/all_to_all | solution.py:9
  191.8 0.7 reduce_sum.49
  (62 shorter events, 2.2 us)
Async XLA Ops:
  7.8 15.6 %all-to-all-start = ((f32[4,1,1]{2,1,0:T(1,128)}), f32[4,1,1]{2,1,0:T(1,128)S(1)}, u32[]{:S(2)}, u32[]{:S(2)}) async-start(f32[4,1,1]{2,1,0:T(1,128)} %broadcast_in_dim.21), calls=%async_computation | async-start | bytes 4096 | tf_op jit(solution)/shard_map/all_to_all | solution.py:9
  54.8 23.4 %all-to-all-start.1 = ((f32[64,1,2048]{2,1,0:T(1,128)}), f32[64,1,2048]{2,1,0:T(1,128)S(1)}, u32[]{:S(2)}, u32[]{:S(2)}) async-start(f32[64,1,2048]{2,1,0:T(1,128)} %broadcast_in_dim.22), calls=%async_computation.1 | async-start | bytes 1048576 | tf_op jit(solution)/shard_map/all_to_all | solution.py:9
  60.6 106.7 %reduce-scatter.2.cloned.1.call-start = ((), (), s32[]{:S(2)}) async-start(), calls=%async_computation.7 | async-start | bytes 10280960 | tf_op jit(solution)/shard_map/reduce_scatter | solution.py:67
  88.3 1.6 copy-start
  108.4 16.0 %all-to-all-start.3 = ((f32[64,1,512]{2,1,0:T(1,128)}), f32[64,1,512]{2,1,0:T(1,128)S(1)}, u32[]{:S(2)}, u32[]{:S(2)}) async-start(f32[64,1,512]{2,1,0:T(1,128)} %broadcast_in_dim.24), calls=%async_computation.4 | async-start | bytes 262144 | tf_op jit(solution)/shard_map/all_to_all | solution.py:9
Sparse Core Ops, SparseCore 0:
  88.4 78.7 reduce-scatter.1
where the time goes:
time: 200 us; the launch traced here: 199 us
  waiting for transfers between devices  69.5 us (35%)
  blocking collectives  68.3 us (34%)
  other arithmetic  25.1 us (13%)
  starting transfers between devices  15.2 us (8%)
  between operations  15 us (8%)
  local copies, waits for them, and re-layouts  6.21 us (3%)
    all_to_all x3, blocking collectives, sent_to_all(): return lax.all_to_all(copies, axis, split_axis=0, concat_axis=0, tiled=True)  68.3 us
    reduce_scatter x1, waiting for transfers between devices, local(): lax.psum_scatter((share * (jnp.exp(block - peak[:, None]) / total[:, None...  42.3 us
    all_to_all x3, waiting for transfers between devices, sent_to_all(): return lax.all_to_all(copies, axis, split_axis=0, concat_axis=0, tiled=True)  27.2 us
    all_to_all x3, starting transfers between devices, sent_to_all(): return lax.all_to_all(copies, axis, split_axis=0, concat_axis=0, tiled=True)  15.2 us
    convert_element_type x1, other arithmetic, local(): (share * (jnp.exp(block - peak[:, None]) / total[:, None])).astype(jnp.bf...  8.62 us
    reduce_sum x1, other arithmetic, local(): jnp.sum(jnp.exp(scores.astype(jnp.float32) - local_peak[:, None]), axis=1)  6.08 us
    reduce_max x1, other arithmetic, local(): local_peak = jnp.max(scores, axis=1).astype(jnp.float32)  4.68 us
  transfers between devices with their start and end apart: 4, of which 3 were waited for; matrix products, arithmetic and copies ran while one was open for 7% of the time, Pallas kernels for 0%

commit v1 on v0

v1 whole, which is shorter than its diff:
```python
import functools

import jax
import jax.numpy as jnp
from jax import lax
from jax.experimental import pallas as pl
from jax.experimental.pallas import tpu as pltpu
from jax.sharding import PartitionSpec as P

MESH = pl.DeviceIdType.MESH
LANES = 128
BLOCK = 48


def over_rows(start, stop, body, carry):
    full = (stop - start) // BLOCK

    def step(i, carry):
        return body(pl.multiple_of(start + i * BLOCK, 16), BLOCK, carry)

    carry = lax.fori_loop(0, full, step, carry)
    rest = start + full * BLOCK
    return body(rest, stop - rest, carry) if rest < stop else carry


def folded(values, combine):
    rows = values.shape[0]
    parts = [values[first : first + 8] for first in range(0, rows - rows % 8, 8)]
    total = functools.reduce(combine, parts) if parts else None
    return total, values[rows - rows % 8 :] if rows % 8 else None


def kernel(
    sizes,
    weight_ref,
    scores,
    student_in,
    out_ref,
    held,
    student,
    opposite,
    near,
    sent_sum,
    got_sum,
    own_pair,
    stats,
    stats_got,
    beside,
    weights,
    final_one,
    final_two,
    local_sem,
    raw_send,
    raw_recv,
    sum_send,
    sum_recv,
    stats_send,
    stats_recv,
    side_send,
    side_recv,
    weight_send,
    weight_recv,
    final_send,
    final_recv,
):
    vocab_rows, tokens, mine, cores, ys, zs = sizes
    half = mine // 2
    x, v = lax.axis_index("teach"), lax.axis_index("vocab")
    plane = ys * cores
    z, y, core = v // plane, lax.rem(v // cores, ys), lax.rem(v, cores)

    def at(z_, y_, core_):
        return {"vocab": (lax.rem(z_, zs) * ys + lax.rem(y_, ys)) * cores + lax.rem(core_, cores)}

    right, left = {"teach": lax.rem(x + 1, 4)}, {"teach": lax.rem(x + 3, 4)}
    sides = (right, left)
    core_peer = at(z, y, core + 1)
    y_peers = (at(z, y + 1, core), at(z, y + ys - 1, core))
    z_peers = (at(z + 1, y, core), at(z + zs - 1, y, core))
    greeted = (right, left, core_peer, *y_peers, *z_peers)

    barrier = pltpu.get_barrier_semaphore()
    for peer in greeted:
        pl.semaphore_signal(barrier, inc=1, device_id=peer, device_id_type=MESH)

    block_copies = []
    for block in range(4):
        columns = pl.ds(block * mine, mine)
        block_copies.append(
            pltpu.make_async_copy(scores.at[:, columns], held.at[:, columns], local_sem.at[block])
        )
    student_copy = pltpu.make_async_copy(student_in, student, local_sem.at[4])
    for copy in (*block_copies, student_copy):
        copy.start()

    pl.semaphore_wait(barrier, len(greeted))

    def remote(source, target, send, recv, peer):
        return pltpu.make_async_remote_copy(
            src_ref=source,
            dst_ref=target,
            send_sem=send,
            recv_sem=recv,
            device_id=peer,
            device_id_type=MESH,
        )

    far = lax.rem(x + 2, 4)
    two_hop_base = (far * mine + half, far * mine)
    next_base = (lax.rem(x + 1, 4) * mine + half, lax.rem(x + 3, 4) * mine)
    one_hop_base = (lax.rem(x + 1, 4) * mine, lax.rem(x + 3, 4) * mine + half)
    pieces = half // LANES

    weights[0] = jnp.full((1, LANES), weight_ref[0], jnp.float32)
    weight_copies = [
        remote(weights.at[0], weights.at[1 + side], weight_send.at[side], weight_recv.at[side], sides[side])
        for side in range(2)
    ]
    for copy in weight_copies:
        copy.start()

    def raw(kind, bases, buffer, piece, side):
        columns = pl.ds(pl.multiple_of(bases[side] + piece * LANES, LANES), LANES)
        slot = (2 * kind + side) * pieces + piece
        return remote(
            scores.at[:, columns],
            buffer.at[side, :, pl.ds(piece * LANES, LANES)],
            raw_send.at[slot],
            raw_recv.at[slot],
            sides[side],
        )

    opposite_copies = [[raw(0, two_hop_base, opposite, p, s) for s in range(2)] for p in range(pieces)]
    near_copies = [[raw(1, one_hop_base, near, p, s) for s in range(2)] for p in range(pieces)]
    for pair in opposite_copies:
        for copy in pair:
            copy.start()
    for pair in near_copies[:-1]:
        for copy in pair:
            copy.start()

    wide = 2 * LANES

    def local_stats(ref, first, count, at_column):
        def one(i, _):
            columns = pl.ds(pl.multiple_of(first + i * wide, LANES), wide)

            def peak_body(row, rows, acc):
                block = ref[pl.ds(row, rows), columns].astype(jnp.float32)
                whole, rest = folded(block, jnp.maximum)
                acc8, acc4 = acc
                if whole is not None:
                    acc8 = jnp.maximum(acc8, whole)
                if rest is not None:
                    acc4 = jnp.maximum(acc4, rest.max(axis=0, keepdims=True))
                return acc8, acc4

            low = jnp.finfo(jnp.float32).min
            acc8, acc4 = over_rows(
                0, vocab_rows, peak_body, (jnp.full((8, wide), low), jnp.full((1, wide), low))
            )
            peak = jnp.maximum(acc8.max(axis=0, keepdims=True), acc4)

            def total_body(row, rows, acc):
                block = jnp.exp(ref[pl.ds(row, rows), columns].astype(jnp.float32) - peak)
                whole, rest = folded(block, jnp.add)
                acc8, acc4 = acc
                if whole is not None:
                    acc8 = acc8 + whole
                if rest is not None:
                    acc4 = acc4 + rest.sum(axis=0, keepdims=True)
                return acc8, acc4

            acc8, acc4 = over_rows(
                0, vocab_rows, total_body, (jnp.zeros((8, wide)), jnp.zeros((1, wide)))
            )
            put = pl.ds(pl.multiple_of(at_column + i * wide, LANES), wide)
            stats[0:1, put] = peak
            stats[1:2, put] = acc8.sum(axis=0, keepdims=True) + acc4
            return 0

        lax.fori_loop(0, count // wide, one, 0)

    student_copy.wait()
    local_stats(student, 0, mine, tokens)
    for block in range(4):
        block_copies[block].wait()
        local_stats(held, block * mine, mine, block * mine)

    def joined(slots):
        peak = stats[0:1]
        for slot in slots:
            peak = jnp.maximum(peak, stats_got[slot, 0:1])
        total = stats[1:2] * jnp.exp(stats[0:1] - peak)
        for slot in slots:
            total = total + stats_got[slot, 1:2] * jnp.exp(stats_got[slot, 0:1] - peak)
        stats[0:1] = peak
        stats[1:2] = total

    def stats_copy(slot, peer, source):
        return remote(source, stats_got.at[slot], stats_send.at[slot], stats_recv.at[slot], peer)

    def round_of(copies):
        for copy in copies:
            copy.start()
        for copy in copies:
            copy.wait()

    round_of([stats_copy(0, core_peer, stats)])
    joined([0])
    round_of([stats_copy(1, y_peers[0], stats), stats_copy(2, y_peers[1], stats)])
    round_of([stats_copy(3, y_peers[0], stats_got.at[1])])
    joined([1, 2, 3])
    round_of([stats_copy(4, z_peers[0], stats), stats_copy(5, z_peers[1], stats)])
    round_of([stats_copy(6, z_peers[0], stats_got.at[4]), stats_copy(7, z_peers[1], stats_got.at[5])])
    round_of([stats_copy(8, z_peers[0], stats_got.at[6]), stats_copy(9, z_peers[1], stats_got.at[7])])
    round_of([stats_copy(10, z_peers[0], stats_got.at[8])])
    joined([4, 5, 6, 7, 8, 9, 10])

    for copy in weight_copies:
        copy.wait()
    relay = remote(weights.at[1], weights.at[3], weight_send.at[2], weight_recv.at[2], right)
    relay.start()
    relay.wait()
    whole_weight = (weights[0] + weights[2]) + (weights[1] + weights[3])
    share = jnp.broadcast_to((weights[0] / whole_weight)[:, 0:1], (1, tokens))

    beside[0, 0:1] = stats[0:1, 0:tokens]
    beside[0, 1:2] = share / stats[1:2, 0:tokens]
    side_copies = [
        remote(beside.at[0], beside.at[1 + side], side_send.at[side], side_recv.at[side], sides[side])
        for side in range(2)
    ]
    for copy in side_copies:
        copy.start()
    for copy in near_copies[-1]:
        copy.start()
    for copy in side_copies:
        copy.wait()

    def term(ref, rows, columns, who, base):
        where = pl.ds(base, LANES)
        peak, factor = beside[who, 0:1, where], beside[who, 1:2, where]
        return jnp.exp(ref[rows, columns].astype(jnp.float32) - peak) * factor

    sum_rows = sent_sum.shape[1]
    cuts = [0, sum_rows // 3, 2 * (sum_rows // 3), sum_rows]

    def sum_copies_of(piece, side):
        columns = pl.ds(piece * LANES, LANES)
        spans = [(0, sum_rows)] if piece < pieces - 1 else list(zip(cuts[:-1], cuts[1:]))
        result = []
        for i, (first, last) in enumerate(spans):
            rows = pl.ds(first, last - first)
            slot = (side * pieces + piece) * 3 + i
            result.append(
                remote(
                    sent_sum.at[side, rows, columns],
                    got_sum.at[side, rows, columns],
                    sum_send.at[slot],
                    sum_recv.at[slot],
                    sides[side],
                )
            )
        return list(zip(spans, result))

    sum_copies = [[sum_copies_of(p, s) for s in range(2)] for p in range(pieces)]
    tail = sum_rows - 16
    sent_sum[:, tail:sum_rows] = jnp.zeros((2, 16, half), jnp.bfloat16)

    for piece in range(pieces):
        for side in range(2):
            opposite_copies[piece][side].wait_recv()
            columns = pl.ds(piece * LANES, LANES)
            base = pl.multiple_of(next_base[side] + piece * LANES, LANES)
            for (first, last), copy in sum_copies[piece][side]:

                def body(row, rows, carry):
                    span = pl.ds(row, rows)
                    total = term(held, span, pl.ds(base, LANES), 0, base) + term(
                        opposite.at[side], span, columns, 1 + side, base
                    )
                    sent_sum[side, span, columns] = total.astype(jnp.bfloat16)
                    return carry

                over_rows(first, min(last, vocab_rows), body, 0)
                copy.start()

    for piece in range(pieces):
        for side in range(2):
            near_copies[piece][side].wait_recv()
            place = side * half + piece * LANES
            base = pl.multiple_of(x * mine + place, LANES)

            def body(row, rows, carry):
                span = pl.ds(row, rows)
                own_pair[span, pl.ds(place, LANES)] = term(held, span, pl.ds(base, LANES), 0, base) + term(
                    near.at[side], span, pl.ds(piece * LANES, LANES), 1 + side, base
                )
                return carry

            over_rows(0, vocab_rows, body, 0)

    student_total = jnp.log(stats[1:2, tokens : tokens + mine])
    for piece in range(pieces):
        for side in range(2):
            place = (1 - side) * half + piece * LANES
            here = pl.ds(place, LANES)
            student_peak = stats[0:1, tokens + place : tokens + place + LANES]
            log_total = student_total[:, place : place + LANES]
            acc = (jnp.zeros((8, LANES)), jnp.zeros((1, LANES)))
            for (first, last), copy in sum_copies[piece][side]:
                copy.wait_recv()

                def body(row, rows, acc):
                    span = pl.ds(row, rows)
                    got = got_sum[side, span, pl.ds(piece * LANES, LANES)].astype(jnp.float32)
                    mixture = own_pair[span, here] + got
                    logq = student[span, here].astype(jnp.float32) - student_peak - log_total
                    value = mixture * (jnp.log(jnp.maximum(mixture, 1e-30)) - logq)
                    whole, rest = folded(value, jnp.add)
                    acc8, acc4 = acc
                    if whole is not None:
                        acc8 = acc8 + whole
                    if rest is not None:
                        acc4 = acc4 + rest.sum(axis=0, keepdims=True)
                    return acc8, acc4

                acc = over_rows(first, min(last, vocab_rows), body, acc)
            final_one[0, :, here] = acc[0].sum(axis=0, keepdims=True) + acc[1]

    mine_in_plane = lax.rem(v, plane)
    first_round = [
        remote(
            final_one.at[0],
            final_one.at[d],
            final_send.at[d],
            final_recv.at[d],
            {"vocab": z * plane + lax.rem(mine_in_plane + d, plane)},
        )
        for d in range(1, plane)
    ]
    for copy in first_round:
        copy.start()
    for copy in first_round:
        copy.wait_recv()
    total = jnp.zeros((1, mine))
    for i in range(plane):
        total = total + final_one[lax.rem(mine_in_plane + plane - i, plane)]
    final_two[0] = total
    second_round = [
        remote(
            final_two.at[0],
            final_two.at[d],
            final_send.at[plane + d],
            final_recv.at[plane + d],
            {"vocab": lax.rem(v + d * plane, zs * plane)},
        )
        for d in range(1, zs)
    ]
    for copy in second_round:
        copy.start()
    for copy in second_round:
        copy.wait_recv()
    total = jnp.zeros((1, mine))
    for i in range(zs):
        total = total + final_two[lax.rem(z + zs - i, zs)]
    out_ref[...] = total

    for copy in (*first_round, *second_round):
        copy.wait_send()
    for piece in range(pieces):
        for side in range(2):
            opposite_copies[piece][side].wait_send()
            near_copies[piece][side].wait_send()
            for _, copy in sum_copies[piece][side]:
                copy.wait_send()


def solution(mesh):
    def local(teacher_logits, teacher_weight, student_logits):
        scores, student = teacher_logits[0].T, student_logits.T
        vocab_rows, tokens = scores.shape
        mine = student.shape[1]
        half = mine // 2
        pieces = half // LANES
        ys, cores = 4, 2
        zs = mesh.shape["vocab"] // (ys * cores)
        sum_rows = -(-vocab_rows // BLOCK) * BLOCK
        together = tokens + mine
        f32, bf16 = jnp.float32, jnp.bfloat16
        dma = pltpu.SemaphoreType.DMA
        out = pl.pallas_call(
            functools.partial(kernel, (vocab_rows, tokens, mine, cores, ys, zs)),
            out_shape=jax.ShapeDtypeStruct((1, mine), f32),
            in_specs=[
                pl.BlockSpec(memory_space=pltpu.SMEM),
                pl.BlockSpec(memory_space=pl.ANY),
                pl.BlockSpec(memory_space=pl.ANY),
            ],
            out_specs=pl.BlockSpec(memory_space=pltpu.VMEM),
            scratch_shapes=[
                pltpu.VMEM((vocab_rows, tokens), bf16),
                pltpu.VMEM((vocab_rows, mine), bf16),
                pltpu.VMEM((2, vocab_rows, half), bf16),
                pltpu.VMEM((2, vocab_rows, half), bf16),
                pltpu.VMEM((2, sum_rows, half), bf16),
                pltpu.VMEM((2, sum_rows, half), bf16),
                pltpu.VMEM((vocab_rows, mine), f32),
                pltpu.VMEM((2, together), f32),
                pltpu.VMEM((11, 2, together), f32),
                pltpu.VMEM((3, 2, tokens), f32),
                pltpu.VMEM((4, 1, LANES), f32),
                pltpu.VMEM((ys * cores, 1, mine), f32),
                pltpu.VMEM((zs, 1, mine), f32),
                dma((5,)),
                dma((4 * pieces,)),
                dma((4 * pieces,)),
                dma((6 * pieces,)),
                dma((6 * pieces,)),
                dma((11,)),
                dma((11,)),
                dma((2,)),
                dma((2,)),
                dma((3,)),
                dma((3,)),
                dma((ys * cores + zs,)),
                dma((ys * cores + zs,)),
            ],
            compiler_params=pltpu.CompilerParams(
                collective_id=0, has_side_effects=True, vmem_limit_bytes=48 * 1024 * 1024
            ),
        )(teacher_weight, scores, student)
        return out.reshape(mine)

    in_specs = (P("teach", "tok", "vocab"), P("teach"), P(("tok", "teach"), "vocab"))
    out_specs = P(("tok", "teach"))
    return jax.shard_map(local, mesh=mesh, in_specs=in_specs, out_specs=out_specs, check_vma=False)
```

time: 200 us -> 91.2 us (0.46)
  Pallas kernels: 0 us -> 88.1 us
  waiting for transfers between devices: 69.5 us -> 0 us
  blocking collectives: 68.3 us -> 0 us
  other arithmetic: 25.1 us -> 0 us
  starting transfers between devices: 15.2 us -> 0 us
  between operations: 15 us -> 0.67 us
  local copies, waits for them, and re-layouts: 6.21 us -> 2.15 us
    pallas_call x0 -> x1, Pallas kernels: none -> 88.1 us  [local(): pl.pallas_call(functools.partial(kernel, (vocab_rows, tokens, mine, cores...]
    all_to_all x3 -> x0, blocking collectives: 68.3 us -> none  [sent_to_all(): return lax.all_to_all(copies, axis, split_axis=0, concat_axis=0, tiled=True)]
    reduce_scatter x1 -> x0, waiting for transfers between devices: 42.3 us -> none  [local(): lax.psum_scatter((share * (jnp.exp(block - peak[:, None]) / total[:, None...]
    all_to_all x3 -> x0, waiting for transfers between devices: 27.2 us -> none  [sent_to_all(): return lax.all_to_all(copies, axis, split_axis=0, concat_axis=0, tiled=True)]
    all_to_all x3 -> x0, starting transfers between devices: 15.2 us -> none  [sent_to_all(): return lax.all_to_all(copies, axis, split_axis=0, concat_axis=0, tiled=True)]
    reduce_sum x5 -> x0, other arithmetic: 11 us -> none  [the longest x1 6.08 us: local(): jnp.sum(jnp.exp(scores.astype(jnp.float32) - local_peak[:, None]), axis=1)]
    convert_element_type x3 -> x0, other arithmetic: 8.63 us -> none  [the longest x1 8.62 us: local(): (share * (jnp.exp(block - peak[:, None]) / total[:, None])).astype(jnp.bf...]
    reduce_max x2 -> x0, other arithmetic: 5.02 us -> none  [the longest x1 4.68 us: local(): local_peak = jnp.max(scores, axis=1).astype(jnp.float32)]
  transfers between devices with their start and end apart: 4 -> 0, of which waited for: 3 -> 0; matrix products, arithmetic and copies ran while one was open for 7% -> 0% of each run, Pallas kernels for 0% -> 0%
where the time goes in v1:
time: 91.2 us; the launch traced here: 90.9 us
  Pallas kernels  88.1 us (97%)
  local copies, waits for them, and re-layouts  2.15 us (2%)
    pallas_call x1, Pallas kernels, local(): pl.pallas_call(functools.partial(kernel, (vocab_rows, tokens, mine, cores...  88.1 us
    unnamed x3, local copies, waits for them, and re-layouts  2.15 us

profile of v1, /device:TPU:1, one launch (start us, length us, event | category | flops | bytes accessed | tf_op | source)
XLA Modules:
  0.0 90.9 jit_solution(10199199979616408298)
XLA Ops:
  0.7 0.0 copy-start
  0.7 1.6 %copy-done = bf16[512,2004]{0,1:T(8,128)(2,1)S(1)} copy-done((bf16[512,2004]{0,1:T(8,128)(2,1)S(1)}, bf16[512,2004]{0,1:T(8,128)(2,1)}, u32[]{:S(2)}) %copy-start) | copy-done | bytes 2052120
  2.2 88.1 %shard_map.37 = f32[1,512]{1,0:T(1,128)S(1)} custom-call(f32[1]{0:T(128)S(6)} %copy.5.weight_ref, bf16[2004,2048]{1,0:T(8,128)(2,1)} %bitcast.7, bf16[2004,512]{1,0:T(8,128)(2,1)S(1)} %bitcast.5), custom_call_target="tpu_custom_call" | custom-call | tf_op jit(solution)/shard_map/pallas_call | solution.py:393
  90.3 0.6 copy.6
Async XLA Ops:
  0.7 1.6 %copy-start = (bf16[512,2004]{0,1:T(8,128)(2,1)S(1)}, bf16[512,2004]{0,1:T(8,128)(2,1)}, u32[]{:S(2)}) copy-start(bf16[512,2004]{0,1:T(8,128)(2,1)} %param.5) | copy-start | bytes 6156292

commit v2 on v1

--- a/solution.py
+++ b/solution.py
@@ -10,6 +10,7 @@
 MESH = pl.DeviceIdType.MESH
 LANES = 128
 BLOCK = 48
+CUTS = (0, 20, 34, 39, 42)
 
 
 def over_rows(start, stop, body, carry):
@@ -32,10 +33,11 @@
 
 def kernel(
     sizes,
-    weight_ref,
+    weight_in,
     scores,
     student_in,
     out_ref,
+    weight,
     held,
     student,
     opposite,
@@ -47,8 +49,7 @@
     stats_got,
     beside,
     weights,
-    final_one,
-    final_two,
+    final,
     local_sem,
     raw_send,
     raw_recv,
@@ -62,6 +63,7 @@
     weight_recv,
     final_send,
     final_recv,
+    known_sem,
 ):
     vocab_rows, tokens, mine, cores, ys, zs = sizes
     half = mine // 2
@@ -90,8 +92,11 @@
             pltpu.make_async_copy(scores.at[:, columns], held.at[:, columns], local_sem.at[block])
         )
     student_copy = pltpu.make_async_copy(student_in, student, local_sem.at[4])
-    for copy in (*block_copies, student_copy):
+    weight_copy = pltpu.make_async_copy(weight_in, weight, local_sem.at[5])
+    for copy in (weight_copy, student_copy, *block_copies):
         copy.start()
+    weight_copy.wait()
+    weights[0] = jnp.full((1, LANES), weight[0], jnp.float32)
 
     pl.semaphore_wait(barrier, len(greeted))
 
@@ -111,7 +116,6 @@
     one_hop_base = (lax.rem(x + 1, 4) * mine, lax.rem(x + 3, 4) * mine + half)
     pieces = half // LANES
 
-    weights[0] = jnp.full((1, LANES), weight_ref[0], jnp.float32)
     weight_copies = [
         remote(weights.at[0], weights.at[1 + side], weight_send.at[side], weight_recv.at[side], sides[side])
         for side in range(2)
@@ -139,6 +143,12 @@
         for copy in pair:
             copy.start()
 
+    def known(stage, peers):
+        for peer in peers:
+            pl.semaphore_signal(known_sem.at[stage], inc=1, device_id=peer, device_id_type=MESH)
+
+    known(0, (core_peer, *y_peers, *z_peers))
+
     wide = 2 * LANES
 
     def local_stats(ref, first, count, at_column):
@@ -183,6 +193,8 @@
 
     student_copy.wait()
     local_stats(student, 0, mine, tokens)
+    pl.semaphore_wait(known_sem.at[0], 5)
+    known(1, (at(z + 2, y, core), at(z + zs - 2, y, core)))
     for block in range(4):
         block_copies[block].wait()
         local_stats(held, block * mine, mine, block * mine)
@@ -208,14 +220,11 @@
 
     round_of([stats_copy(0, core_peer, stats)])
     joined([0])
-    round_of([stats_copy(1, y_peers[0], stats), stats_copy(2, y_peers[1], stats)])
-    round_of([stats_copy(3, y_peers[0], stats_got.at[1])])
+    round_of([stats_copy(d, at(z, y + d, core), stats) for d in (2, 1, 3)])
     joined([1, 2, 3])
-    round_of([stats_copy(4, z_peers[0], stats), stats_copy(5, z_peers[1], stats)])
-    round_of([stats_copy(6, z_peers[0], stats_got.at[4]), stats_copy(7, z_peers[1], stats_got.at[5])])
-    round_of([stats_copy(8, z_peers[0], stats_got.at[6]), stats_copy(9, z_peers[1], stats_got.at[7])])
-    round_of([stats_copy(10, z_peers[0], stats_got.at[8])])
-    joined([4, 5, 6, 7, 8, 9, 10])
+    pl.semaphore_wait(known_sem.at[1], 2)
+    round_of([stats_copy(3 + d, at(z + d, y, core), stats) for d in (4, 3, 5, 2, 6, 1, 7)])
+    joined(range(4, 11))
 
     for copy in weight_copies:
         copy.wait()
@@ -244,7 +253,7 @@
         return jnp.exp(ref[rows, columns].astype(jnp.float32) - peak) * factor
 
     sum_rows = sent_sum.shape[1]
-    cuts = [0, sum_rows // 3, 2 * (sum_rows // 3), sum_rows]
+    cuts = [cut * (sum_rows // CUTS[-1]) for cut in CUTS]
 
     def sum_copies_of(piece, side):
         columns = pl.ds(piece * LANES, LANES)
@@ -252,7 +261,7 @@
         result = []
         for i, (first, last) in enumerate(spans):
             rows = pl.ds(first, last - first)
-            slot = (side * pieces + piece) * 3 + i
+            slot = (side * pieces + piece) * (len(cuts) - 1) + i
             result.append(
                 remote(
                     sent_sum.at[side, rows, columns],
@@ -301,74 +310,72 @@
 
             over_rows(0, vocab_rows, body, 0)
 
+    def hops(d):
+        dz, dy = d // plane, d // cores % ys
+        return min(dz, zs - dz) + min(dy, ys - dy)
+
+    others = sorted(range(1, zs * plane), key=lambda d: -hops(d))
+
+    def spread(piece):
+        for d in others:
+            dz, dy, dc = d // plane, d // cores % ys, d % cores
+            remote(
+                final.at[piece, v],
+                final.at[piece, v],
+                final_send.at[piece],
+                final_recv.at[piece],
+                at(z + dz, y + dy, core + dc),
+            ).start()
+
+    def spread_done(piece):
+        every = final.at[piece, pl.ds(0, len(others))]
+        return pltpu.make_async_copy(every, every, final_recv.at[piece]), pltpu.make_async_copy(
+            every, every, final_send.at[piece]
+        )
+
     student_total = jnp.log(stats[1:2, tokens : tokens + mine])
-    for piece in range(pieces):
+
+    def divergence_part(piece, side, first, last, acc):
+        place = (1 - side) * half + piece * LANES
+        here = pl.ds(place, LANES)
+        student_peak = stats[0:1, tokens + place : tokens + place + LANES]
+        log_total = student_total[:, place : place + LANES]
+
+        def body(row, rows, acc):
+            span = pl.ds(row, rows)
+            got = got_sum[side, span, pl.ds(piece * LANES, LANES)].astype(jnp.float32)
+            mixture = own_pair[span, here] + got
+            logq = student[span, here].astype(jnp.float32) - student_peak - log_total
+            value = mixture * (jnp.log(jnp.maximum(mixture, 1e-30)) - logq)
+            whole, rest = folded(value, jnp.add)
+            acc8, acc4 = acc
+            if whole is not None:
+                acc8 = acc8 + whole
+            if rest is not None:
+                acc4 = acc4 + rest.sum(axis=0, keepdims=True)
+            return acc8, acc4
+
+        return over_rows(first, min(last, vocab_rows), body, acc)
+
+    for piece in range(pieces):
+        accs = [(jnp.zeros((8, LANES)), jnp.zeros((1, LANES)))] * 2
+        for both in zip(*sum_copies[piece]):
+            for side, ((first, last), copy) in enumerate(both):
+                copy.wait_recv()
+                accs[side] = divergence_part(piece, side, first, last, accs[side])
         for side in range(2):
-            place = (1 - side) * half + piece * LANES
-            here = pl.ds(place, LANES)
-            student_peak = stats[0:1, tokens + place : tokens + place + LANES]
-            log_total = student_total[:, place : place + LANES]
-            acc = (jnp.zeros((8, LANES)), jnp.zeros((1, LANES)))
-            for (first, last), copy in sum_copies[piece][side]:
-                copy.wait_recv()
-
-                def body(row, rows, acc):
-                    span = pl.ds(row, rows)
-                    got = got_sum[side, span, pl.ds(piece * LANES, LANES)].astype(jnp.float32)
-                    mixture = own_pair[span, here] + got
-                    logq = student[span, here].astype(jnp.float32) - student_peak - log_total
-                    value = mixture * (jnp.log(jnp.maximum(mixture, 1e-30)) - logq)
-                    whole, rest = folded(value, jnp.add)
-                    acc8, acc4 = acc
-                    if whole is not None:
-                        acc8 = acc8 + whole
-                    if rest is not None:
-                        acc4 = acc4 + rest.sum(axis=0, keepdims=True)
-                    return acc8, acc4
-
-                acc = over_rows(first, min(last, vocab_rows), body, acc)
-            final_one[0, :, here] = acc[0].sum(axis=0, keepdims=True) + acc[1]
-
-    mine_in_plane = lax.rem(v, plane)
-    first_round = [
-        remote(
-            final_one.at[0],
-            final_one.at[d],
-            final_send.at[d],
-            final_recv.at[d],
-            {"vocab": z * plane + lax.rem(mine_in_plane + d, plane)},
-        )
-        for d in range(1, plane)
-    ]
-    for copy in first_round:
-        copy.start()
-    for copy in first_round:
-        copy.wait_recv()
-    total = jnp.zeros((1, mine))
-    for i in range(plane):
-        total = total + final_one[lax.rem(mine_in_plane + plane - i, plane)]
-    final_two[0] = total
-    second_round = [
-        remote(
-            final_two.at[0],
-            final_two.at[d],
-            final_send.at[plane + d],
-            final_recv.at[plane + d],
-            {"vocab": lax.rem(v + d * plane, zs * plane)},
-        )
-        for d in range(1, zs)
-    ]
-    for copy in second_round:
-        copy.start()
-    for copy in second_round:
-        copy.wait_recv()
-    total = jnp.zeros((1, mine))
-    for i in range(zs):
-        total = total + final_two[lax.rem(z + zs - i, zs)]
-    out_ref[...] = total
-
-    for copy in (*first_round, *second_round):
-        copy.wait_send()
+            part = accs[side][0].sum(axis=0, keepdims=True) + accs[side][1]
+            final[piece, v, :, (1 - side) * LANES : (2 - side) * LANES] = part
+        spread(piece)
+    for piece in range(pieces):
+        spread_done(piece)[0].wait()
+        total = final[piece].sum(axis=0)
+        for part in range(2):
+            place = part * half + piece * LANES
+            out_ref[:, place : place + LANES] = total[:, part * LANES : (part + 1) * LANES]
+
+    for piece in range(pieces):
+        spread_done(piece)[1].wait()
     for piece in range(pieces):
         for side in range(2):
             opposite_copies[piece][side].wait_send()
@@ -385,7 +392,8 @@
         half = mine // 2
         pieces = half // LANES
         ys, cores = 4, 2
-        zs = mesh.shape["vocab"] // (ys * cores)
+        everyone = mesh.shape["vocab"]
+        zs = everyone // (ys * cores)
         sum_rows = -(-vocab_rows // BLOCK) * BLOCK
         together = tokens + mine
         f32, bf16 = jnp.float32, jnp.bfloat16
@@ -394,12 +402,13 @@
             functools.partial(kernel, (vocab_rows, tokens, mine, cores, ys, zs)),
             out_shape=jax.ShapeDtypeStruct((1, mine), f32),
             in_specs=[
-                pl.BlockSpec(memory_space=pltpu.SMEM),
+                pl.BlockSpec(memory_space=pl.ANY),
                 pl.BlockSpec(memory_space=pl.ANY),
                 pl.BlockSpec(memory_space=pl.ANY),
             ],
             out_specs=pl.BlockSpec(memory_space=pltpu.VMEM),
             scratch_shapes=[
+                pltpu.SMEM((1,), f32),
                 pltpu.VMEM((vocab_rows, tokens), bf16),
                 pltpu.VMEM((vocab_rows, mine), bf16),
                 pltpu.VMEM((2, vocab_rows, half), bf16),
@@ -411,24 +420,24 @@
                 pltpu.VMEM((11, 2, together), f32),
                 pltpu.VMEM((3, 2, tokens), f32),
                 pltpu.VMEM((4, 1, LANES), f32),
-                pltpu.VMEM((ys * cores, 1, mine), f32),
-                pltpu.VMEM((zs, 1, mine), f32),
-                dma((5,)),
+                pltpu.VMEM((pieces, everyone, 1, 2 * LANES), f32),
+                dma((6,)),
                 dma((4 * pieces,)),
                 dma((4 * pieces,)),
-                dma((6 * pieces,)),
-                dma((6 * pieces,)),
+                dma((2 * pieces * (len(CUTS) - 1),)),
+                dma((2 * pieces * (len(CUTS) - 1),)),
                 dma((11,)),
                 dma((11,)),
                 dma((2,)),
                 dma((2,)),
                 dma((3,)),
                 dma((3,)),
-                dma((ys * cores + zs,)),
-                dma((ys * cores + zs,)),
+                dma((pieces,)),
+                dma((pieces,)),
+                pltpu.SemaphoreType.REGULAR((2,)),
             ],
             compiler_params=pltpu.CompilerParams(
-                collective_id=0, has_side_effects=True, vmem_limit_bytes=48 * 1024 * 1024
+                collective_id=0, has_side_effects=True, vmem_limit_bytes=60 * 1024 * 1024
             ),
         )(teacher_weight, scores, student)
         return out.reshape(mine)

time: 91.2 us -> 88.3 us (0.968)
  Pallas kernels: 88.1 us -> 86.3 us
    pallas_call x1, Pallas kernels: 88.1 us -> 86.3 us  [local(): pl.pallas_call(functools.partial(kernel, (vocab_rows, tokens, mine, cores...]
    unnamed x3 -> x1, local copies, waits for them, and re-layouts: 2.15 us -> 1.26 us
where the time goes in v2:
time: 88.3 us; the launch traced here: 88.2 us
  Pallas kernels  86.3 us (98%)
  local copies, waits for them, and re-layouts  1.26 us (1%)
    pallas_call x1, Pallas kernels, local(): pl.pallas_call(functools.partial(kernel, (vocab_rows, tokens, mine, cores...  86.3 us

profile of v2, /device:TPU:1, one launch (start us, length us, event | category | flops | bytes accessed | tf_op | source)
XLA Modules:
  0.0 88.2 jit_solution(4155820570882299916)
XLA Ops:
  0.7 86.3 %shard_map.37 = f32[1,512]{1,0:T(1,128)} custom-call(f32[1]{0:T(128)S(6)} %copy.5.weight_in, bf16[2004,2048]{1,0:T(8,128)(2,1)} %bitcast.5, bf16[2004,512]{1,0:T(8,128)(2,1)} %bitcast.6), custom_call_target="tpu_custom_call" | custom-call | tf_op jit(solution)/shard_map/pallas_call | solution.py:401
  87.0 1.3 %copy.6 = f32[512]{0:T(512)} copy(f32[512]{0:T(512)} %bitcast.7) | data formatting | bytes 4096

commit v3 on v2

--- a/solution.py
+++ b/solution.py
@@ -9,7 +9,8 @@
 
 MESH = pl.DeviceIdType.MESH
 LANES = 128
-BLOCK = 48
+BLOCK = 240
+CUT = 48
 CUTS = (0, 20, 34, 39, 42)
 
 
@@ -24,20 +25,20 @@
     return body(rest, stop - rest, carry) if rest < stop else carry
 
 
-def folded(values, combine):
+def folded(values, combine, group=8):
     rows = values.shape[0]
-    parts = [values[first : first + 8] for first in range(0, rows - rows % 8, 8)]
+    left = rows % group
+    parts = [values[first : first + group] for first in range(0, rows - left, group)]
     total = functools.reduce(combine, parts) if parts else None
-    return total, values[rows - rows % 8 :] if rows % 8 else None
+    return total, values[rows - left :] if left else None
 
 
 def kernel(
     sizes,
-    weight_in,
+    weight,
     scores,
     student_in,
     out_ref,
-    weight,
     held,
     student,
     opposite,
@@ -92,10 +93,8 @@
             pltpu.make_async_copy(scores.at[:, columns], held.at[:, columns], local_sem.at[block])
         )
     student_copy = pltpu.make_async_copy(student_in, student, local_sem.at[4])
-    weight_copy = pltpu.make_async_copy(weight_in, weight, local_sem.at[5])
-    for copy in (weight_copy, student_copy, *block_copies):
+    for copy in (student_copy, *block_copies):
         copy.start()
-    weight_copy.wait()
     weights[0] = jnp.full((1, LANES), weight[0], jnp.float32)
 
     pl.semaphore_wait(barrier, len(greeted))
@@ -156,20 +155,19 @@
             columns = pl.ds(pl.multiple_of(first + i * wide, LANES), wide)
 
             def peak_body(row, rows, acc):
-                block = ref[pl.ds(row, rows), columns].astype(jnp.float32)
-                whole, rest = folded(block, jnp.maximum)
+                whole, rest = folded(ref[pl.ds(row, rows), columns], jnp.maximum, 16)
                 acc8, acc4 = acc
                 if whole is not None:
                     acc8 = jnp.maximum(acc8, whole)
                 if rest is not None:
-                    acc4 = jnp.maximum(acc4, rest.max(axis=0, keepdims=True))
+                    acc4 = jnp.maximum(acc4, rest.astype(jnp.float32).max(axis=0, keepdims=True))
                 return acc8, acc4
 
-            low = jnp.finfo(jnp.float32).min
+            low = -1e30
             acc8, acc4 = over_rows(
-                0, vocab_rows, peak_body, (jnp.full((8, wide), low), jnp.full((1, wide), low))
+                0, vocab_rows, peak_body, (jnp.full((16, wide), low, ref.dtype), jnp.full((1, wide), low))
             )
-            peak = jnp.maximum(acc8.max(axis=0, keepdims=True), acc4)
+            peak = jnp.maximum(acc8.astype(jnp.float32).max(axis=0, keepdims=True), acc4)
 
             def total_body(row, rows, acc):
                 block = jnp.exp(ref[pl.ds(row, rows), columns].astype(jnp.float32) - peak)
@@ -327,11 +325,9 @@
                 at(z + dz, y + dy, core + dc),
             ).start()
 
-    def spread_done(piece):
+    def spread_done(piece, semaphore):
         every = final.at[piece, pl.ds(0, len(others))]
-        return pltpu.make_async_copy(every, every, final_recv.at[piece]), pltpu.make_async_copy(
-            every, every, final_send.at[piece]
-        )
+        pltpu.make_async_copy(every, every, semaphore.at[piece]).wait()
 
     student_total = jnp.log(stats[1:2, tokens : tokens + mine])
 
@@ -368,14 +364,14 @@
             final[piece, v, :, (1 - side) * LANES : (2 - side) * LANES] = part
         spread(piece)
     for piece in range(pieces):
-        spread_done(piece)[0].wait()
+        spread_done(piece, final_recv)
         total = final[piece].sum(axis=0)
         for part in range(2):
             place = part * half + piece * LANES
             out_ref[:, place : place + LANES] = total[:, part * LANES : (part + 1) * LANES]
 
     for piece in range(pieces):
-        spread_done(piece)[1].wait()
+        spread_done(piece, final_send)
     for piece in range(pieces):
         for side in range(2):
             opposite_copies[piece][side].wait_send()
@@ -394,21 +390,20 @@
         ys, cores = 4, 2
         everyone = mesh.shape["vocab"]
         zs = everyone // (ys * cores)
-        sum_rows = -(-vocab_rows // BLOCK) * BLOCK
+        sum_rows = -(-vocab_rows // CUT) * CUT
         together = tokens + mine
         f32, bf16 = jnp.float32, jnp.bfloat16
         dma = pltpu.SemaphoreType.DMA
         out = pl.pallas_call(
             functools.partial(kernel, (vocab_rows, tokens, mine, cores, ys, zs)),
-            out_shape=jax.ShapeDtypeStruct((1, mine), f32),
+            out_shape=pltpu.VMEM((1, mine), f32),
             in_specs=[
-                pl.BlockSpec(memory_space=pl.ANY),
-                pl.BlockSpec(memory_space=pl.ANY),
-                pl.BlockSpec(memory_space=pl.ANY),
+                pl.BlockSpec(memory_space=pltpu.SMEM),
+                pl.BlockSpec(memory_space=pltpu.HBM),
+                pl.BlockSpec(memory_space=pltpu.HBM),
             ],
             out_specs=pl.BlockSpec(memory_space=pltpu.VMEM),
             scratch_shapes=[
-                pltpu.SMEM((1,), f32),
                 pltpu.VMEM((vocab_rows, tokens), bf16),
                 pltpu.VMEM((vocab_rows, mine), bf16),
                 pltpu.VMEM((2, vocab_rows, half), bf16),
@@ -421,7 +416,7 @@
                 pltpu.VMEM((3, 2, tokens), f32),
                 pltpu.VMEM((4, 1, LANES), f32),
                 pltpu.VMEM((pieces, everyone, 1, 2 * LANES), f32),
-                dma((6,)),
+                dma((5,)),
                 dma((4 * pieces,)),
                 dma((4 * pieces,)),
                 dma((2 * pieces * (len(CUTS) - 1),)),
@@ -439,7 +434,7 @@
             compiler_params=pltpu.CompilerParams(
                 collective_id=0, has_side_effects=True, vmem_limit_bytes=60 * 1024 * 1024
             ),
-        )(teacher_weight, scores, student)
+        )(teacher_weight, *(pltpu.with_memory_space_constraint(a, pltpu.HBM) for a in (scores, student)))
         return out.reshape(mine)
 
     in_specs = (P("teach", "tok", "vocab"), P("teach"), P(("tok", "teach"), "vocab"))

time: 88.3 us -> 87 us (0.985)
  no operation moved by 1% of the time
where the time goes in v3:
time: 87 us; the launch traced here: 86.9 us
  Pallas kernels  85.6 us (98%)
    pallas_call x1, Pallas kernels, local(): pl.pallas_call(functools.partial(kernel, (vocab_rows, tokens, mine, cores...  85.6 us

profile of v3, /device:TPU:1, one launch (start us, length us, event | category | flops | bytes accessed | tf_op | source)
XLA Modules:
  0.0 86.9 jit_solution(9683700070239582817)
XLA Ops:
  0.7 85.6 %shard_map.37 = f32[1,512]{1,0:T(1,128)S(1)} custom-call(f32[1]{0:T(128)S(6)} %copy.6.weight, bf16[2004,2048]{1,0:T(8,128)(2,1)} %bitcast.6, bf16[2004,512]{1,0:T(8,128)(2,1)} %bitcast.7), custom_call_target="tpu_custom_call" | custom-call | tf_op jit(solution)/shard_map/pallas_call | solution.py:397
  86.3 0.6 copy.5

commit v4 on v3

--- a/solution.py
+++ b/solution.py
@@ -10,8 +10,8 @@
 MESH = pl.DeviceIdType.MESH
 LANES = 128
 BLOCK = 240
-CUT = 48
-CUTS = (0, 20, 34, 39, 42)
+CUTS = (0, 960, 1632, 1872)
+GIVEN = 64
 
 
 def over_rows(start, stop, body, carry):
@@ -51,6 +51,13 @@
     beside,
     weights,
     final,
+    extra,
+    extra_student,
+    extra_opposite,
+    extra_near,
+    extra_sent,
+    extra_got,
+    extra_pair,
     local_sem,
     raw_send,
     raw_recv,
@@ -65,6 +72,10 @@
     final_send,
     final_recv,
     known_sem,
+    give_send,
+    give_recv,
+    extra_send,
+    extra_recv,
 ):
     vocab_rows, tokens, mine, cores, ys, zs = sizes
     half = mine // 2
@@ -80,11 +91,28 @@
     core_peer = at(z, y, core + 1)
     y_peers = (at(z, y + 1, core), at(z, y + ys - 1, core))
     z_peers = (at(z + 1, y, core), at(z + zs - 1, y, core))
-    greeted = (right, left, core_peer, *y_peers, *z_peers)
+    takes = z < zs // 2 - 1
+    gives = (z >= zs // 2) & (z < zs - 1)
+    keeps = jnp.logical_not(gives)
+    half_way = at(z + zs // 2, y, core)
 
     barrier = pltpu.get_barrier_semaphore()
-    for peer in greeted:
+
+    def greet(peer):
         pl.semaphore_signal(barrier, inc=1, device_id=peer, device_id_type=MESH)
+
+    def along(place, size, next_peer, first_to_last, act):
+        pl.when(place < size - 1)(lambda: act(next_peer))
+        pl.when(place == 0)(lambda: act(first_to_last))
+
+    def waited_for(place, size):
+        return (place + size - 2) // (size - 1) + place // (size - 1)
+
+    for peer in (right, left, core_peer):
+        greet(peer)
+    along(y, ys, y_peers[0], y_peers[1], greet)
+    along(z, zs, z_peers[0], z_peers[1], greet)
+    before = waited_for(y, ys) + waited_for(z, zs)
 
     block_copies = []
     for block in range(4):
@@ -97,7 +125,7 @@
         copy.start()
     weights[0] = jnp.full((1, LANES), weight[0], jnp.float32)
 
-    pl.semaphore_wait(barrier, len(greeted))
+    pl.semaphore_wait(barrier, 3 + before)
 
     def remote(source, target, send, recv, peer):
         return pltpu.make_async_remote_copy(
@@ -122,16 +150,42 @@
     for copy in weight_copies:
         copy.start()
 
+    class Either:
+        def __init__(self, make, first, last):
+            self.whole = make(first, last)
+            self.less = make(GIVEN, last) if first < GIVEN else None
+
+        def do(self, act):
+            if self.less is None:
+                act(self.whole)
+            else:
+                pl.when(keeps)(lambda: act(self.whole))
+                pl.when(gives)(lambda: act(self.less))
+
+        def start(self):
+            self.do(lambda copy: copy.start())
+
+        def wait_recv(self):
+            self.do(lambda copy: copy.wait_recv())
+
+        def wait_send(self):
+            self.do(lambda copy: copy.wait_send())
+
     def raw(kind, bases, buffer, piece, side):
         columns = pl.ds(pl.multiple_of(bases[side] + piece * LANES, LANES), LANES)
         slot = (2 * kind + side) * pieces + piece
-        return remote(
-            scores.at[:, columns],
-            buffer.at[side, :, pl.ds(piece * LANES, LANES)],
-            raw_send.at[slot],
-            raw_recv.at[slot],
-            sides[side],
-        )
+
+        def make(first, last):
+            rows = pl.ds(first, last - first)
+            return remote(
+                scores.at[rows, columns],
+                buffer.at[side, rows, pl.ds(piece * LANES, LANES)],
+                raw_send.at[slot],
+                raw_recv.at[slot],
+                sides[side],
+            )
+
+        return Either(make, 0, vocab_rows)
 
     opposite_copies = [[raw(0, two_hop_base, opposite, p, s) for s in range(2)] for p in range(pieces)]
     near_copies = [[raw(1, one_hop_base, near, p, s) for s in range(2)] for p in range(pieces)]
@@ -146,7 +200,12 @@
         for peer in peers:
             pl.semaphore_signal(known_sem.at[stage], inc=1, device_id=peer, device_id_type=MESH)
 
-    known(0, (core_peer, *y_peers, *z_peers))
+    def answer(place, size, last_peer, last_to_first):
+        pl.when(place > 0)(lambda: known(0, (last_peer,)))
+        pl.when(place == size - 1)(lambda: known(0, (last_to_first,)))
+
+    answer(y, ys, y_peers[1], y_peers[0])
+    answer(z, zs, z_peers[1], z_peers[0])
 
     wide = 2 * LANES
 
@@ -191,11 +250,14 @@
 
     student_copy.wait()
     local_stats(student, 0, mine, tokens)
-    pl.semaphore_wait(known_sem.at[0], 5)
-    known(1, (at(z + 2, y, core), at(z + zs - 2, y, core)))
+    pl.when(before < 4)(lambda: pl.semaphore_wait(known_sem.at[0], 4 - before))
+    known(1, (*y_peers, *z_peers))
     for block in range(4):
         block_copies[block].wait()
         local_stats(held, block * mine, mine, block * mine)
+        if block == 1:
+            pl.semaphore_wait(known_sem.at[1], 4)
+            known(2, (at(z + 2, y, core), at(z + zs - 2, y, core)))
 
     def joined(slots):
         peak = stats[0:1]
@@ -220,9 +282,20 @@
     joined([0])
     round_of([stats_copy(d, at(z, y + d, core), stats) for d in (2, 1, 3)])
     joined([1, 2, 3])
-    pl.semaphore_wait(known_sem.at[1], 2)
+    pl.semaphore_wait(known_sem.at[2], 2)
     round_of([stats_copy(3 + d, at(z + d, y, core), stats) for d in (4, 3, 5, 2, 6, 1, 7)])
     joined(range(4, 11))
+
+    given_rows = pl.ds(0, GIVEN)
+    give_copies = [
+        remote(scores.at[given_rows], extra, give_send.at[0], give_recv.at[0], half_way),
+        remote(student_in.at[given_rows], extra_student, give_send.at[1], give_recv.at[1], half_way),
+    ]
+
+    @pl.when(gives)
+    def _():
+        for copy in give_copies:
+            copy.start()
 
     for copy in weight_copies:
         copy.wait()
@@ -245,35 +318,74 @@
     for copy in side_copies:
         copy.wait()
 
-    def term(ref, rows, columns, who, base):
-        where = pl.ds(base, LANES)
+    def term(ref, rows, columns, who, base, width=LANES):
+        where = pl.ds(base, width)
         peak, factor = beside[who, 0:1, where], beside[who, 1:2, where]
         return jnp.exp(ref[rows, columns].astype(jnp.float32) - peak) * factor
 
-    sum_rows = sent_sum.shape[1]
-    cuts = [cut * (sum_rows // CUTS[-1]) for cut in CUTS]
+    cuts = [*CUTS, vocab_rows]
 
     def sum_copies_of(piece, side):
         columns = pl.ds(piece * LANES, LANES)
-        spans = [(0, sum_rows)] if piece < pieces - 1 else list(zip(cuts[:-1], cuts[1:]))
+        spans = [(0, vocab_rows)] if piece < pieces - 1 else list(zip(cuts[:-1], cuts[1:]))
         result = []
         for i, (first, last) in enumerate(spans):
-            rows = pl.ds(first, last - first)
             slot = (side * pieces + piece) * (len(cuts) - 1) + i
-            result.append(
-                remote(
+
+            def make(first, last):
+                rows = pl.ds(first, last - first)
+                return remote(
                     sent_sum.at[side, rows, columns],
                     got_sum.at[side, rows, columns],
                     sum_send.at[slot],
                     sum_recv.at[slot],
                     sides[side],
                 )
+
+            result.append(Either(make, first, last))
+        return list(zip(spans, result))
+
+    sum_copies = [[sum_copies_of(p, s) for s in range(2)] for p in range(pieces)]
+
+    def extra_copy(kind, side, source, target):
+        slot = 2 * kind + side
+        return remote(source, target, extra_send.at[slot], extra_recv.at[slot], sides[side])
+
+    def of_extra(bases, side):
+        return extra.at[:, pl.ds(pl.multiple_of(bases[side], LANES), half)]
+
+    extra_raw = [
+        extra_copy(kind, side, of_extra(bases, side), buffer.at[side])
+        for kind, (bases, buffer) in enumerate(((two_hop_base, extra_opposite), (one_hop_base, extra_near)))
+        for side in range(2)
+    ]
+    extra_sums = [extra_copy(2, side, extra_sent.at[side], extra_got.at[side]) for side in range(2)]
+    every = pl.ds(0, GIVEN)
+
+    def send_extra_raw():
+        for copy in give_copies:
+            copy.wait_recv()
+        for copy in extra_raw:
+            copy.start()
+
+    def send_extra_sums():
+        for side in range(2):
+            extra_raw[side].wait_recv()
+            base = pl.multiple_of(next_base[side], LANES)
+            total = term(extra, every, pl.ds(base, half), 0, base, half) + term(
+                extra_opposite.at[side], every, pl.ds(0, half), 1 + side, base, half
             )
-        return list(zip(spans, result))
-
-    sum_copies = [[sum_copies_of(p, s) for s in range(2)] for p in range(pieces)]
-    tail = sum_rows - 16
-    sent_sum[:, tail:sum_rows] = jnp.zeros((2, 16, half), jnp.bfloat16)
+            extra_sent[side] = total.astype(jnp.bfloat16)
+            extra_sums[side].start()
+
+    def add_extra_pair():
+        for side in range(2):
+            extra_raw[2 + side].wait_recv()
+            place = side * half
+            base = pl.multiple_of(x * mine + place, LANES)
+            extra_pair[:, place : place + half] = term(extra, every, pl.ds(base, half), 0, base, half) + term(
+                extra_near.at[side], every, pl.ds(0, half), 1 + side, base, half
+            )
 
     for piece in range(pieces):
         for side in range(2):
@@ -290,8 +402,9 @@
                     sent_sum[side, span, columns] = total.astype(jnp.bfloat16)
                     return carry
 
-                over_rows(first, min(last, vocab_rows), body, 0)
+                over_rows(first, last, body, 0)
                 copy.start()
+        pl.when(takes)(send_extra_raw if piece == 0 else send_extra_sums)
 
     for piece in range(pieces):
         for side in range(2):
@@ -307,6 +420,7 @@
                 return carry
 
             over_rows(0, vocab_rows, body, 0)
+    pl.when(takes)(add_extra_pair)
 
     def hops(d):
         dz, dy = d // plane, d // cores % ys
@@ -331,18 +445,20 @@
 
     student_total = jnp.log(stats[1:2, tokens : tokens + mine])
 
+    def divergences(pair, got, logits, place, width):
+        mixture = pair + got.astype(jnp.float32)
+        student_peak = stats[0:1, tokens + place : tokens + place + width]
+        logq = logits.astype(jnp.float32) - student_peak - student_total[:, place : place + width]
+        return mixture * (jnp.log(jnp.maximum(mixture, 1e-30)) - logq)
+
     def divergence_part(piece, side, first, last, acc):
         place = (1 - side) * half + piece * LANES
         here = pl.ds(place, LANES)
-        student_peak = stats[0:1, tokens + place : tokens + place + LANES]
-        log_total = student_total[:, place : place + LANES]
 
         def body(row, rows, acc):
             span = pl.ds(row, rows)
-            got = got_sum[side, span, pl.ds(piece * LANES, LANES)].astype(jnp.float32)
-            mixture = own_pair[span, here] + got
-            logq = student[span, here].astype(jnp.float32) - student_peak - log_total
-            value = mixture * (jnp.log(jnp.maximum(mixture, 1e-30)) - logq)
+            got = got_sum[side, span, pl.ds(piece * LANES, LANES)]
+            value = divergences(own_pair[span, here], got, student[span, here], place, LANES)
             whole, rest = folded(value, jnp.add)
             acc8, acc4 = acc
             if whole is not None:
@@ -351,18 +467,42 @@
                 acc4 = acc4 + rest.sum(axis=0, keepdims=True)
             return acc8, acc4
 
-        return over_rows(first, min(last, vocab_rows), body, acc)
+        return over_rows(first, last, body, acc)
+
+    def add_extra_divergence():
+        for side in range(2):
+            extra_sums[side].wait_recv()
+            place = (1 - side) * half
+            here = pl.ds(place, half)
+            value = divergences(extra_pair[:, here], extra_got[side], extra_student[:, here], place, half)
+            part = value.sum(axis=0, keepdims=True)
+            for piece in range(pieces):
+                lanes = slice((1 - side) * LANES, (2 - side) * LANES)
+                final[piece, v, :, lanes] = final[piece, v, :, lanes] + part[:, piece * LANES : (piece + 1) * LANES]
 
     for piece in range(pieces):
         accs = [(jnp.zeros((8, LANES)), jnp.zeros((1, LANES)))] * 2
         for both in zip(*sum_copies[piece]):
             for side, ((first, last), copy) in enumerate(both):
                 copy.wait_recv()
+                if first == 0:
+                    head, rest = divergence_part(piece, side, 0, GIVEN, accs[side])
+                    accs[side] = jnp.where(gives, 0.0, head), rest
+                    first = GIVEN
                 accs[side] = divergence_part(piece, side, first, last, accs[side])
         for side in range(2):
             part = accs[side][0].sum(axis=0, keepdims=True) + accs[side][1]
             final[piece, v, :, (1 - side) * LANES : (2 - side) * LANES] = part
-        spread(piece)
+        if piece < pieces - 1:
+            pl.when(jnp.logical_not(takes))(functools.partial(spread, piece))
+
+    @pl.when(takes)
+    def _():
+        add_extra_divergence()
+        for piece in range(pieces - 1):
+            spread(piece)
+
+    spread(pieces - 1)
     for piece in range(pieces):
         spread_done(piece, final_recv)
         total = final[piece].sum(axis=0)
@@ -378,6 +518,16 @@
             near_copies[piece][side].wait_send()
             for _, copy in sum_copies[piece][side]:
                 copy.wait_send()
+
+    @pl.when(takes)
+    def _():
+        for copy in (*extra_raw, *extra_sums):
+            copy.wait_send()
+
+    @pl.when(gives)
+    def _():
+        for copy in give_copies:
+            copy.wait_send()
 
 
 def solution(mesh):
@@ -390,7 +540,6 @@
         ys, cores = 4, 2
         everyone = mesh.shape["vocab"]
         zs = everyone // (ys * cores)
-        sum_rows = -(-vocab_rows // CUT) * CUT
         together = tokens + mine
         f32, bf16 = jnp.float32, jnp.bfloat16
         dma = pltpu.SemaphoreType.DMA
@@ -408,19 +557,26 @@
                 pltpu.VMEM((vocab_rows, mine), bf16),
                 pltpu.VMEM((2, vocab_rows, half), bf16),
                 pltpu.VMEM((2, vocab_rows, half), bf16),
-                pltpu.VMEM((2, sum_rows, half), bf16),
-                pltpu.VMEM((2, sum_rows, half), bf16),
+                pltpu.VMEM((2, vocab_rows, half), bf16),
+                pltpu.VMEM((2, vocab_rows, half), bf16),
                 pltpu.VMEM((vocab_rows, mine), f32),
                 pltpu.VMEM((2, together), f32),
                 pltpu.VMEM((11, 2, together), f32),
                 pltpu.VMEM((3, 2, tokens), f32),
                 pltpu.VMEM((4, 1, LANES), f32),
                 pltpu.VMEM((pieces, everyone, 1, 2 * LANES), f32),
+                pltpu.VMEM((GIVEN, tokens), bf16),
+                pltpu.VMEM((GIVEN, mine), bf16),
+                pltpu.VMEM((2, GIVEN, half), bf16),
+                pltpu.VMEM((2, GIVEN, half), bf16),
+                pltpu.VMEM((2, GIVEN, half), bf16),
+                pltpu.VMEM((2, GIVEN, half), bf16),
+                pltpu.VMEM((GIVEN, mine), f32),
                 dma((5,)),
                 dma((4 * pieces,)),
                 dma((4 * pieces,)),
-                dma((2 * pieces * (len(CUTS) - 1),)),
-                dma((2 * pieces * (len(CUTS) - 1),)),
+                dma((2 * pieces * len(CUTS),)),
+                dma((2 * pieces * len(CUTS),)),
                 dma((11,)),
                 dma((11,)),
                 dma((2,)),
@@ -429,7 +585,11 @@
                 dma((3,)),
                 dma((pieces,)),
                 dma((pieces,)),
-                pltpu.SemaphoreType.REGULAR((2,)),
+                pltpu.SemaphoreType.REGULAR((3,)),
+                dma((2,)),
+                dma((2,)),
+                dma((6,)),
+                dma((6,)),
             ],
             compiler_params=pltpu.CompilerParams(
                 collective_id=0, has_side_effects=True, vmem_limit_bytes=60 * 1024 * 1024

time: 87 us -> 85.8 us (0.986)
  Pallas kernels: 85.6 us -> 84.4 us
    pallas_call x1, Pallas kernels: 85.6 us -> 84.4 us  [local(): pl.pallas_call(functools.partial(kernel, (vocab_rows, tokens, mine, cores...]
where the time goes in v4:
time: 85.8 us; the launch traced here: 85.7 us
  Pallas kernels  84.4 us (98%)
    pallas_call x1, Pallas kernels, local(): pl.pallas_call(functools.partial(kernel, (vocab_rows, tokens, mine, cores...  84.4 us

profile of v4, /device:TPU:1, one launch (start us, length us, event | category | flops | bytes accessed | tf_op | source)
XLA Modules:
  0.0 85.7 jit_solution(2426794590148100450)
XLA Ops:
  0.7 84.4 %shard_map.37 = f32[1,512]{1,0:T(1,128)S(1)} custom-call(f32[1]{0:T(128)S(6)} %copy.6.weight, bf16[2004,2048]{1,0:T(8,128)(2,1)} %bitcast.6, bf16[2004,512]{1,0:T(8,128)(2,1)} %bitcast.7), custom_call_target="tpu_custom_call" | custom-call | tf_op jit(solution)/shard_map/pallas_call | solution.py:546
  85.1 0.6 copy.5

commit v5 on v4

--- a/solution.py
+++ b/solution.py
@@ -58,6 +58,7 @@
     extra_sent,
     extra_got,
     extra_pair,
+    extra_part,
     local_sem,
     raw_send,
     raw_recv,
@@ -92,9 +93,11 @@
     y_peers = (at(z, y + 1, core), at(z, y + ys - 1, core))
     z_peers = (at(z + 1, y, core), at(z + zs - 1, y, core))
     takes = z < zs // 2 - 1
-    gives = (z >= zs // 2) & (z < zs - 1)
+    gives = z >= zs // 2
     keeps = jnp.logical_not(gives)
-    half_way = at(z + zs // 2, y, core)
+    takes_set = (takes, z == 0)
+    gives_set = (gives & (z < zs - 1), z == zs - 1)
+    taker = (at(z + zs // 2, y, core), at(z + 1, y, core))
 
     barrier = pltpu.get_barrier_semaphore()
 
@@ -288,14 +291,22 @@
 
     given_rows = pl.ds(0, GIVEN)
     give_copies = [
-        remote(scores.at[given_rows], extra, give_send.at[0], give_recv.at[0], half_way),
-        remote(student_in.at[given_rows], extra_student, give_send.at[1], give_recv.at[1], half_way),
+        [
+            remote(source.at[given_rows], target.at[e], give_send.at[2 * e + i], give_recv.at[2 * e + i], taker[e])
+            for i, (source, target) in enumerate(((scores, extra), (student_in, extra_student)))
+        ]
+        for e in range(2)
     ]
 
-    @pl.when(gives)
-    def _():
-        for copy in give_copies:
+    def each_set(predicates, act):
+        for e in range(2):
+            pl.when(predicates[e])(functools.partial(act, e))
+
+    def start_giving(e):
+        for copy in give_copies[e]:
             copy.start()
+
+    each_set(gives_set, start_giving)
 
     for copy in weight_copies:
         copy.wait()
@@ -347,52 +358,60 @@
 
     sum_copies = [[sum_copies_of(p, s) for s in range(2)] for p in range(pieces)]
 
-    def extra_copy(kind, side, source, target):
-        slot = 2 * kind + side
+    extra_part[...] = jnp.zeros_like(extra_part)
+
+    def extra_copy(e, kind, side, source, target):
+        slot = 6 * e + 2 * kind + side
         return remote(source, target, extra_send.at[slot], extra_recv.at[slot], sides[side])
 
-    def of_extra(bases, side):
-        return extra.at[:, pl.ds(pl.multiple_of(bases[side], LANES), half)]
+    def of_extra(e, bases, side):
+        return extra.at[e, :, pl.ds(pl.multiple_of(bases[side], LANES), half)]
 
     extra_raw = [
-        extra_copy(kind, side, of_extra(bases, side), buffer.at[side])
-        for kind, (bases, buffer) in enumerate(((two_hop_base, extra_opposite), (one_hop_base, extra_near)))
-        for side in range(2)
+        [
+            extra_copy(e, kind, side, of_extra(e, bases, side), buffer.at[e, side])
+            for kind, (bases, buffer) in enumerate(((two_hop_base, extra_opposite), (one_hop_base, extra_near)))
+            for side in range(2)
+        ]
+        for e in range(2)
     ]
-    extra_sums = [extra_copy(2, side, extra_sent.at[side], extra_got.at[side]) for side in range(2)]
+    extra_sums = [
+        [extra_copy(e, 2, side, extra_sent.at[e, side], extra_got.at[e, side]) for side in range(2)] for e in range(2)
+    ]
     every = pl.ds(0, GIVEN)
 
-    def send_extra_raw():
-        for copy in give_copies:
+    def send_extra_raw(e):
+        for copy in give_copies[e]:
             copy.wait_recv()
-        for copy in extra_raw:
+        for copy in extra_raw[e]:
             copy.start()
 
-    def send_extra_sums():
+    def send_extra_sums(e):
         for side in range(2):
-            extra_raw[side].wait_recv()
+            extra_raw[e][side].wait_recv()
             base = pl.multiple_of(next_base[side], LANES)
-            total = term(extra, every, pl.ds(base, half), 0, base, half) + term(
-                extra_opposite.at[side], every, pl.ds(0, half), 1 + side, base, half
+            total = term(extra.at[e], every, pl.ds(base, half), 0, base, half) + term(
+                extra_opposite.at[e, side], every, pl.ds(0, half), 1 + side, base, half
             )
-            extra_sent[side] = total.astype(jnp.bfloat16)
-            extra_sums[side].start()
-
-    def add_extra_pair():
+            extra_sent[e, side] = total.astype(jnp.bfloat16)
+            extra_sums[e][side].start()
+
+    def add_extra_pair(e):
         for side in range(2):
-            extra_raw[2 + side].wait_recv()
+            extra_raw[e][2 + side].wait_recv()
             place = side * half
             base = pl.multiple_of(x * mine + place, LANES)
-            extra_pair[:, place : place + half] = term(extra, every, pl.ds(base, half), 0, base, half) + term(
-                extra_near.at[side], every, pl.ds(0, half), 1 + side, base, half
+            extra_pair[e, :, place : place + half] = term(extra.at[e], every, pl.ds(base, half), 0, base, half) + term(
+                extra_near.at[e, side], every, pl.ds(0, half), 1 + side, base, half
             )
 
     for piece in range(pieces):
         for side in range(2):
             opposite_copies[piece][side].wait_recv()
-            columns = pl.ds(piece * LANES, LANES)
-            base = pl.multiple_of(next_base[side] + piece * LANES, LANES)
-            for (first, last), copy in sum_copies[piece][side]:
+        for i, both in enumerate(zip(*sum_copies[piece])):
+            for side, ((first, last), copy) in enumerate(both):
+                columns = pl.ds(piece * LANES, LANES)
+                base = pl.multiple_of(next_base[side] + piece * LANES, LANES)
 
                 def body(row, rows, carry):
                     span = pl.ds(row, rows)
@@ -404,7 +423,10 @@
 
                 over_rows(first, last, body, 0)
                 copy.start()
-        pl.when(takes)(send_extra_raw if piece == 0 else send_extra_sums)
+            if piece == 0:
+                each_set(takes_set, send_extra_raw)
+            elif piece == pieces - 1 and i == 0:
+                each_set(takes_set, send_extra_sums)
 
     for piece in range(pieces):
         for side in range(2):
@@ -420,7 +442,7 @@
                 return carry
 
             over_rows(0, vocab_rows, body, 0)
-    pl.when(takes)(add_extra_pair)
+    each_set(takes_set, add_extra_pair)
 
     def hops(d):
         dz, dy = d // plane, d // cores % ys
@@ -469,20 +491,22 @@
 
         return over_rows(first, last, body, acc)
 
-    def add_extra_divergence():
+    def add_extra_divergence(e):
         for side in range(2):
-            extra_sums[side].wait_recv()
+            extra_sums[e][side].wait_recv()
             place = (1 - side) * half
             here = pl.ds(place, half)
-            value = divergences(extra_pair[:, here], extra_got[side], extra_student[:, here], place, half)
-            part = value.sum(axis=0, keepdims=True)
-            for piece in range(pieces):
-                lanes = slice((1 - side) * LANES, (2 - side) * LANES)
-                final[piece, v, :, lanes] = final[piece, v, :, lanes] + part[:, piece * LANES : (piece + 1) * LANES]
+            value = divergences(extra_pair[e, :, here], extra_got[e, side], extra_student[e, :, here], place, half)
+            extra_part[:, here] = extra_part[:, here] + value.sum(axis=0, keepdims=True)
+
+    def add_extra_part(piece, side):
+        lanes = pl.ds((1 - side) * LANES, LANES)
+        place = (1 - side) * half + piece * LANES
+        final[piece, v, :, lanes] = final[piece, v, :, lanes] + extra_part[:, place : place + LANES]
 
     for piece in range(pieces):
         accs = [(jnp.zeros((8, LANES)), jnp.zeros((1, LANES)))] * 2
-        for both in zip(*sum_copies[piece]):
+        for i, both in enumerate(zip(*sum_copies[piece])):
             for side, ((first, last), copy) in enumerate(both):
                 copy.wait_recv()
                 if first == 0:
@@ -490,18 +514,23 @@
                     accs[side] = jnp.where(gives, 0.0, head), rest
                     first = GIVEN
                 accs[side] = divergence_part(piece, side, first, last, accs[side])
+            if piece == pieces - 1 and i == 1:
+
+                each_set(takes_set, add_extra_divergence)
+
+                @pl.when(takes)
+                def _():
+                    for side in range(2):
+                        add_extra_part(0, side)
+                    spread(0)
+
         for side in range(2):
             part = accs[side][0].sum(axis=0, keepdims=True) + accs[side][1]
             final[piece, v, :, (1 - side) * LANES : (2 - side) * LANES] = part
-        if piece < pieces - 1:
-            pl.when(jnp.logical_not(takes))(functools.partial(spread, piece))
-
-    @pl.when(takes)
-    def _():
-        add_extra_divergence()
-        for piece in range(pieces - 1):
-            spread(piece)
-
+            if piece > 0:
+                add_extra_part(piece, side)
+        if piece == 0:
+            pl.when(jnp.logical_not(takes))(functools.partial(spread, 0))
     spread(pieces - 1)
     for piece in range(pieces):
         spread_done(piece, final_recv)
@@ -519,15 +548,16 @@
             for _, copy in sum_copies[piece][side]:
                 copy.wait_send()
 
-    @pl.when(takes)
-    def _():
-        for copy in (*extra_raw, *extra_sums):
+    def extra_sent_out(e):
+        for copy in (*extra_raw[e], *extra_sums[e]):
             copy.wait_send()
 
-    @pl.when(gives)
-    def _():
-        for copy in give_copies:
+    def given(e):
+        for copy in give_copies[e]:
             copy.wait_send()
+
+    each_set(takes_set, extra_sent_out)
+    each_set(gives_set, given)
 
 
 def solution(mesh):
@@ -565,13 +595,14 @@
                 pltpu.VMEM((3, 2, tokens), f32),
                 pltpu.VMEM((4, 1, LANES), f32),
                 pltpu.VMEM((pieces, everyone, 1, 2 * LANES), f32),
-                pltpu.VMEM((GIVEN, tokens), bf16),
-                pltpu.VMEM((GIVEN, mine), bf16),
-                pltpu.VMEM((2, GIVEN, half), bf16),
-                pltpu.VMEM((2, GIVEN, half), bf16),
-                pltpu.VMEM((2, GIVEN, half), bf16),
-                pltpu.VMEM((2, GIVEN, half), bf16),
-                pltpu.VMEM((GIVEN, mine), f32),
+                pltpu.VMEM((2, GIVEN, tokens), bf16),
+                pltpu.VMEM((2, GIVEN, mine), bf16),
+                pltpu.VMEM((2, 2, GIVEN, half), bf16),
+                pltpu.VMEM((2, 2, GIVEN, half), bf16),
+                pltpu.VMEM((2, 2, GIVEN, half), bf16),
+                pltpu.VMEM((2, 2, GIVEN, half), bf16),
+                pltpu.VMEM((2, GIVEN, mine), f32),
+                pltpu.VMEM((1, mine), f32),
                 dma((5,)),
                 dma((4 * pieces,)),
                 dma((4 * pieces,)),
@@ -586,10 +617,10 @@
                 dma((pieces,)),
                 dma((pieces,)),
                 pltpu.SemaphoreType.REGULAR((3,)),
-                dma((2,)),
-                dma((2,)),
-                dma((6,)),
-                dma((6,)),
+                dma((4,)),
+                dma((4,)),
+                dma((12,)),
+                dma((12,)),
             ],
             compiler_params=pltpu.CompilerParams(
                 collective_id=0, has_side_effects=True, vmem_limit_bytes=60 * 1024 * 1024

time: 85.8 us -> 85.4 us (level)
  no operation moved by 1% of the time
where the time goes in v5:
time: 85.4 us
  Pallas kernels  84.1 us (98%)
    pallas_call x1, Pallas kernels, local(): pl.pallas_call(functools.partial(kernel, (vocab_rows, tokens, mine, cores...  84.1 us

profile of v5, /device:TPU:1, one launch (start us, length us, event | category | flops | bytes accessed | tf_op | source)
XLA Modules:
  0.0 85.4 jit_solution(10409627626823370840)
XLA Ops:
  0.7 84.1 %shard_map.37 = f32[1,512]{1,0:T(1,128)S(1)} custom-call(f32[1]{0:T(128)S(6)} %copy.6.weight, bf16[2004,2048]{1,0:T(8,128)(2,1)} %bitcast.6, bf16[2004,512]{1,0:T(8,128)(2,1)} %bitcast.7), custom_call_target="tpu_custom_call" | custom-call | tf_op jit(solution)/shard_map/pallas_call | solution.py:576
  84.8 0.6 copy.5
